TPU v7x, 512 devices: a whole 4x8x8 slice. The times are simulated.
512 devices in a mesh: dp: 16 (over z_lo, y), mp: 8 (over z_hi, core), section: 4 (over x).
Axes of the slice: x: 4, y: 8, z: 8 (z_hi: 4, z_lo: 2; z = z_hi * 2 + z_lo), core: 2. Of those that a mesh axis runs over, the one named last changes fastest.
Arguments:
- states: bfloat16 [16384, 8192], P(('dp', 'section'), 'mp'), may hold values from -6 to 6
- direction: bfloat16 [16384, 1024], P(('dp', 'section'), 'mp'), may hold values from -0.09375 to 0.09375
- old_logp: bfloat16 [16384], P(('dp', 'section')), may hold values from -4 to -0.049804688
- lengths: int32 [128], P(('dp', 'section')), may hold values from 1 to 128, as said below
- group_ids: int32 [128], P(('dp', 'section')), may hold values from 0 to 15, as said below
- routes: int32 [16384, 1], P(('dp', 'section')), may hold values from 0 to 15; in each aligned block of 256 rows (0 to 255, 256 to 511, ...) at most 20 rows name the same one
- reward_head: bfloat16 [8192], P('mp'), may hold values from -0.0625 to 0.0625
- policy_k: bfloat16 [8192, 1024], P(('dp', 'section'), 'mp'), may hold values from -0.0625 to 0.0625
- reference_k: bfloat16 [8192, 1024], P(('dp', 'section'), 'mp'), may hold values from -0.0625 to 0.0625
Outputs:
- grad_k: float32 [8192, 1024], P(('dp', 'section'), 'mp')
- packed_logp: float32 [16, 4, 320], P('dp', 'section')
Inputs may be any that keep to these rules, and one draw needn't show every extreme that they name: `lengths`: some response has all 128 tokens valid. `group_ids`: each prompt id is held by exactly 8 responses. `routes`: among the rows of one rollout device at most 20 name the same learner shard, a bound that some block reaches of them.
All inputs are finite; a program needn't handle non-finite values.
Results may differ from a plain program's by a relative error of at most 0.004.
Values may be sent and summed in bfloat16 or wider, within the bound.
No kernel may reach another device: no remote copies, remote signals or barrier semaphores. Data moves between devices by JAX's collectives and lax.ppermute only.
A program may use at most 64 MiB of HBM per device.

v0:
```python
import jax
import jax.numpy as jnp
from jax import lax
from jax.sharding import PartitionSpec as P

GROUP = 8
kl_weight = 0.4
var_offset = 0.25


def row_slots(routes, shards, capacity):
    target = routes[:, 0]
    choose = (target[:, None] == jnp.arange(shards, dtype=jnp.int32)[None, :]).astype(jnp.int32)
    ranked = jnp.cumsum(choose, axis=0) - 1
    within = jnp.sum(ranked * choose, axis=1)
    places = target * capacity + within
    row_count = routes.shape[0]
    source = jnp.full((shards * capacity,), row_count, jnp.int32)
    return source.at[places].set(jnp.arange(row_count, dtype=jnp.int32))


def pick_rows(values, source):
    return jnp.take(values, source, axis=0, mode="fill", fill_value=0)


def advantages(scores, lengths, group_ids):
    seq_count = lengths.shape[0]
    seq_len = scores.shape[0] // seq_count
    groups = seq_count * lax.axis_size("dp") * lax.axis_size("section") // GROUP
    valid = (jnp.arange(seq_len, dtype=jnp.int32)[None, :] < lengths[:, None]).astype(jnp.float32)
    reward = jnp.sum(scores.reshape(seq_count, seq_len) * valid, axis=1) / jnp.sqrt(
        lengths.astype(jnp.float32)
    )
    member = (group_ids[:, None] == jnp.arange(groups, dtype=jnp.int32)[None, :]).astype(
        jnp.float32
    )
    totals, squares = lax.psum(
        (
            jnp.sum(member * reward[:, None], axis=0),
            jnp.sum(member * (reward * reward)[:, None], axis=0),
        ),
        ("dp", "section"),
    )
    center = totals / GROUP
    spread = squares / GROUP - center * center
    own_center = jnp.sum(member * center[None, :], axis=1)
    own_spread = jnp.sum(member * spread[None, :], axis=1)
    advantage = ((reward - own_center) / jnp.sqrt(own_spread + var_offset)).astype(jnp.bfloat16)
    return (jnp.repeat(advantage, seq_len), valid.reshape(-1))


def project(whole, policy_k, reference_k):
    return (
        jnp.dot(
            whole,
            lax.all_gather(policy_k, ("dp", "section"), axis=0, tiled=True),
            preferred_element_type=jnp.float32,
        ),
        jnp.dot(
            whole,
            lax.all_gather(reference_k, ("dp", "section"), axis=0, tiled=True),
            preferred_element_type=jnp.float32,
        ),
    )


def token_coef(dir_rows, old_rows, adv_rows, valid_rows, term_policy, term_reference):
    logp = old_rows.astype(jnp.float32) + term_policy
    coef = valid_rows * (
        -adv_rows * jnp.exp(term_policy) + kl_weight * (1.0 - jnp.exp(term_reference - term_policy))
    )
    change = (coef[:, None] * dir_rows.astype(jnp.float32)).astype(jnp.bfloat16)
    return (logp, change)


def weight_grads(whole, change):
    return lax.psum_scatter(
        lax.dot_general(
            whole, change, (((0,), (0,)), ((), ())), preferred_element_type=jnp.float32
        ),
        ("dp", "section"),
        scatter_dimension=0,
        tiled=True,
    )


def body(
    states, direction, old_logp, lengths, group_ids, routes, reward_head, policy_k, reference_k
):
    row_count = states.shape[0]
    score_part = jnp.dot(states, reward_head, preferred_element_type=jnp.float32)
    shards = lax.axis_size("dp")
    capacity = max(2, 5 * row_count // (4 * shards))
    source = row_slots(routes, shards, capacity)
    scores = lax.psum(score_part, "mp")
    adv_rows, valid_rows = advantages(scores, lengths, group_ids)
    extras = jnp.stack([old_logp, adv_rows, valid_rows.astype(jnp.bfloat16)], axis=1)
    send_states = pick_rows(states, source).reshape(shards, capacity, states.shape[1])
    send_dir = pick_rows(direction, source).reshape(shards, capacity, direction.shape[1])
    send_extras = pick_rows(extras, source).reshape(shards, capacity, 3)
    got_states, got_dir, got_extras = (
        lax.all_to_all(send_states, "dp", split_axis=0, concat_axis=0, tiled=True),
        lax.all_to_all(send_dir, "dp", split_axis=0, concat_axis=0, tiled=True),
        lax.all_to_all(send_extras, "dp", split_axis=0, concat_axis=0, tiled=True),
    )
    slot_count = shards * capacity
    learn_states = got_states.reshape(slot_count, states.shape[1])
    learn_dir = got_dir.reshape(slot_count, direction.shape[1])
    learn_extras = got_extras.reshape(slot_count, 3)
    whole = lax.all_gather(learn_states, "mp", axis=1, tiled=True)
    key_policy, key_reference = project(whole, policy_k, reference_k)
    dir_wide = learn_dir.astype(jnp.float32)
    term_policy, term_reference = lax.psum(
        (jnp.sum(dir_wide * key_policy, axis=1), jnp.sum(dir_wide * key_reference, axis=1)), "mp"
    )
    logp, change = token_coef(
        learn_dir,
        learn_extras[:, 0],
        learn_extras[:, 1].astype(jnp.float32),
        learn_extras[:, 2].astype(jnp.float32),
        term_policy,
        term_reference,
    )
    grad_k = weight_grads(whole, change)
    packed_logp = logp.reshape(1, 1, slot_count)
    return (grad_k, packed_logp)


def solution(mesh):
    return jax.shard_map(
        body,
        mesh=mesh,
        in_specs=(
            P(("dp", "section"), "mp"),
            P(("dp", "section"), "mp"),
            P(("dp", "section")),
            P(("dp", "section")),
            P(("dp", "section")),
            P(("dp", "section"), None),
            P("mp"),
            P(("dp", "section"), "mp"),
            P(("dp", "section"), "mp"),
        ),
        out_specs=(P(("dp", "section"), "mp"), P("dp", "section", None)),
        check_vma=False,
    )
```

profile of v0, /device:TPU:64, one launch (start us, length us, event | category | flops | bytes accessed | tf_op | source)
XLA Modules:
  0.0 1203.8 jit_solution(4523003245266882236)
XLA Ops:
  7.2 0.7 all-gather.6.cloned.1.call-update
  8.0 0.7 fusion.6
  8.6 0.6 reduce-window.6
  9.2 0.2 slice_reduce_fusion
  9.4 0.8 fusion.5
  10.2 0.7 compare_select_fusion
  10.9 1.4 scatter_custom_fusion
  12.4 2.1 gather_fusion
  14.5 0.1 gather.19
  14.9 29.1 %all_to_all.15 = bf16[16,20,1024]{2,1,0:T(8,128)(2,1)S(1)} all-to-all(bf16[16,20,1024]{2,1,0:T(8,128)(2,1)S(1)} %broadcast_select_fusion), channel_id=1, replica_groups=mesh['dp'=16,'mp'=8,'section'=4] {'dp'}, dimensions={0} | all-to-all | bytes 1310720 | tf_op jit(solution)/shard_map/all_to_all | solution.py:102
  44.0 1.0 reshape.105
  45.0 0.7 all-gather.8.cloned.1.call-update
  45.7 1.4 gather_fusion.2
  47.2 0.8 broadcast_select_fusion.1
  47.9 6.3 all-to-all-start.2
  54.4 0.2 fusion.16
  54.7 7.0 all-to-all-done.2
  61.7 253.6 %all-gather.6.cloned.1.call-done = bf16[8192,128]{1,0:T(8,128)(2,1)} async-done(((bf16[128,128]{1,0:T(8,128)(2,1)}), bf16[8192,128]{1,0:T(8,128)(2,1)}) %all-gather.6.cloned.1.call-update) | async-done | bytes 2097168 | tf_op jit(solution)/shard_map/all_gather | solution.py:56
  315.3 65.4 %all-gather.4.cloned.1.call-done = bf16[320,8192]{1,0:T(8,128)(2,1)} async-done(((bf16[320,1024]{1,0:T(8,128)(2,1)}), bf16[320,8192]{1,0:T(8,128)(2,1)}) %all-gather.4.cloned.1.call-update) | async-done | bytes 5242896 | tf_op jit(solution)/shard_map/all_gather | solution.py:110
  380.7 4.8 fusion
  385.5 297.1 %all-gather.8.cloned.1.call-done = bf16[8192,128]{1,0:T(8,128)(2,1)} async-done(((bf16[128,128]{1,0:T(8,128)(2,1)}), bf16[8192,128]{1,0:T(8,128)(2,1)}) %all-gather.8.cloned.1.call-update) | async-done | bytes 2097168 | tf_op jit(solution)/shard_map/all_gather | solution.py:61
  682.6 4.8 fusion.1
  687.4 14.7 %all-reduce.1 = (f32[2,128]{1,0:T(2,128)S(1)}, f32[320]{0:T(512)S(1)}, f32[320]{0:T(512)S(1)}) all-reduce(f32[2,128]{1,0:T(2,128)S(1)} %bitcast.47, f32[320]{0:T(512)S(1)} %fusion.1, f32[320]{0:T(512)S(1)} %fusion), channel_id=1, replica_groups=mesh['dp'=16,'mp'=8,'section'=4] {'mp'}, use_global_device_ids=true, to_apply=%region_4.5 | all-reduce | flops 896 | bytes 7168 | tf_op jit(solution)/shard_map/psum | solution.py:95
  702.1 0.2 select_reduce_fusion.4
  702.4 157.2 %all-reduce = (f32[16]{0:T(128)S(1)}, f32[16]{0:T(128)S(1)}) all-reduce(f32[16]{0:T(128)S(1)} %get-tuple-element.7, f32[16]{0:T(128)S(1)} %get-tuple-element.8), channel_id=1, replica_groups=mesh['dp'=16,'mp'=8,'section'=4] {'dp','section'}, use_global_device_ids=true, to_apply=%region_7.8 | all-reduce | flops 32 | bytes 256 | tf_op jit(solution)/shard_map/psum | solution.py:37
  859.6 0.2 select_reduce_fusion.2
  859.9 0.1 copy.22
  860.1 1.4 gather_fusion.1
  861.7 10.8 all_to_all.16
  872.7 6.5 fusion.2
  879.1 0.6 reshape.108
  879.7 317.5 %reduce-scatter.2.cloned.1.call-done = f32[128,128]{1,0:T(8,128)} async-done(((f32[8192,128]{1,0:T(8,128)}), f32[128,128]{1,0:T(8,128)}) %reduce-scatter.2.cloned.1.call-update) | async-done | bytes 65552 | tf_op jit(solution)/shard_map/reduce_scatter | solution.py:77
  (46 shorter events, 1.2 us)
Async XLA Ops:
  7.2 5.2 copy-start
  7.2 308.1 %all-gather.6.cloned.1.call-start = ((), (), s32[]{:S(2)}) async-start(), calls=%async_computation.5 | async-start | bytes 2129920 | tf_op jit(solution)/shard_map/all_gather | solution.py:56
  7.9 372.8 %all-gather.4.cloned.1.call-start = ((), (), s32[]{:S(2)}) async-start(), calls=%async_computation.4 | async-start | bytes 5898240 | tf_op jit(solution)/shard_map/all_gather | solution.py:110
  12.3 33.4 %copy-start.1 = (bf16[256,128]{1,0:T(8,128)(2,1)S(1)}, bf16[256,128]{1,0:T(8,128)(2,1)}, u32[]{:S(2)}) copy-start(bf16[256,128]{1,0:T(8,128)(2,1)} %param.10) | copy-start | bytes 196612
  14.5 39.9 %copy-start.2 = (bf16[1024]{0:T(1024)(128)(2,1)S(1)}, bf16[1024]{0:T(1024)(128)(2,1)}, u32[]{:S(2)}) copy-start(bf16[1024]{0:T(1024)(128)(2,1)} %param.15) | copy-start | bytes 6148
  14.5 39.9 %copy-start.5 = (bf16[256]{0:T(256)(128)(2,1)S(1)}, bf16[256]{0:T(256)(128)(2,1)}, u32[]{:S(2)}) copy-start(bf16[256]{0:T(256)(128)(2,1)} %param.11) | copy-start | bytes 1540
  14.5 40.1 %copy-start.4 = (s32[2]{0:T(128)S(1)}, s32[2]{0:T(128)}, u32[]{:S(2)}) copy-start(s32[2]{0:T(128)} %param.12) | copy-start | bytes 28
  45.0 637.6 %all-gather.8.cloned.1.call-start = ((), (), s32[]{:S(2)}) async-start(), calls=%async_computation.6 | async-start | bytes 2129920 | tf_op jit(solution)/shard_map/all_gather | solution.py:61
  47.9 13.8 %all-to-all-start.2 = ((bf16[16,20,128]{2,1,0:T(8,128)(2,1)}), bf16[16,20,128]{2,1,0:T(8,128)(2,1)S(1)}, u32[]{:S(2)}, u32[]{:S(2)}) async-start(bf16[16,20,128]{2,1,0:T(8,128)(2,1)} %broadcast_select_fusion.1), calls=%async_computation.2 | async-start | bytes 196608 | tf_op jit(solution)/shard_map/all_to_all | solution.py:103
  54.3 1143.0 %reduce-scatter.2.cloned.1.call-start = ((), (), s32[]{:S(2)}) async-start(), calls=%async_computation.7 | async-start | bytes 4259840 | tf_op jit(solution)/shard_map/reduce_scatter | solution.py:77
  385.5 316.8 %copy-start.3 = (s32[2]{0:T(128)S(1)}, s32[2]{0:T(128)}, u32[]{:S(2)}) copy-start(s32[2]{0:T(128)} %param.13) | copy-start | bytes 28
Sparse Core Ops, SparseCore 0:
  10.1 305.1 all-gather.5
  317.4 63.2 all-gather.3
  382.8 299.7 all-gather.7
  879.3 317.9 reduce-scatter.1
where the time goes:
time: 1200 us
  waiting for transfers between devices  942 us (78%)
  blocking collectives  212 us (18%)
  matrix products  16.2 us (1%)
  between operations  14 us (1%)
    reduce_scatter x1, waiting for transfers between devices, weight_grads(): lax.psum_scatter(lax.dot_general(whole, change, (((0,), (0,)), ((), ())),...  318 us
    all_gather x1, waiting for transfers between devices, project(): lax.all_gather(reference_k, ('dp', 'section'), axis=0, tiled=True)  297 us
    all_gather x1, waiting for transfers between devices, project(): lax.all_gather(policy_k, ('dp', 'section'), axis=0, tiled=True)  254 us
    psum x1, blocking collectives, advantages(): lax.psum((jnp.sum(member * reward[:, None], axis=0), jnp.sum(member * (re...  157 us
    all_gather x1, waiting for transfers between devices, body(): whole = lax.all_gather(learn_states, 'mp', axis=1, tiled=True)  65.4 us
    all_to_all x1, blocking collectives, body(): lax.all_to_all(send_states, 'dp', split_axis=0, concat_axis=0, tiled=True)  29.1 us
  transfers between devices with their start and end apart: 5, of which 5 were waited for; matrix products, arithmetic and copies ran while one was open for 1% of the time, Pallas kernels for 0%

commit v1 on v0

--- a/solution.py
+++ b/solution.py
@@ -34,12 +34,12 @@
     member = (group_ids[:, None] == jnp.arange(groups, dtype=jnp.int32)[None, :]).astype(
         jnp.float32
     )
-    totals, squares = lax.psum(
+    name_steps_all = lambda z: lax.psum(lax.psum(z, "section"), "dp")
+    totals, squares = name_steps_all(
         (
             jnp.sum(member * reward[:, None], axis=0),
             jnp.sum(member * (reward * reward)[:, None], axis=0),
-        ),
-        ("dp", "section"),
+        )
     )
     center = totals / GROUP
     spread = squares / GROUP - center * center

time: 1200 us -> 1090 us (0.908)
  the two profiles are of different devices: /device:TPU:64 before, /device:TPU:128 now
where the time goes in v1:
time: 1090 us
  waiting for transfers between devices  944 us (87%)
  blocking collectives  97.5 us (9%)
  matrix products  16.2 us (1%)
  between operations  14 us (1%)
    reduce_scatter x1, waiting for transfers between devices, weight_grads(): lax.psum_scatter(lax.dot_general(whole, change, (((0,), (0,)), ((), ())),...  320 us
    all_gather x1, waiting for transfers between devices, project(): lax.all_gather(reference_k, ('dp', 'section'), axis=0, tiled=True)  298 us
    all_gather x1, waiting for transfers between devices, project(): lax.all_gather(policy_k, ('dp', 'section'), axis=0, tiled=True)  253 us
    all_gather x1, waiting for transfers between devices, body(): whole = lax.all_gather(learn_states, 'mp', axis=1, tiled=True)  64.4 us
    psum x2, blocking collectives, advantages(): name_steps_all = lambda z: lax.psum(lax.psum(z, 'section'), 'dp')  43.6 us
    all_to_all x1, blocking collectives, body(): lax.all_to_all(send_states, 'dp', split_axis=0, concat_axis=0, tiled=True)  30.2 us
  transfers between devices with their start and end apart: 5, of which 5 were waited for; matrix products, arithmetic and copies ran while one was open for 1% of the time, Pallas kernels for 0%

profile of v1, /device:TPU:128, one launch (start us, length us, event | category | flops | bytes accessed | tf_op | source)
XLA Modules:
  0.0 1091.3 jit_solution(8042205743395202685)
XLA Ops:
  7.2 0.7 all-gather.6.cloned.1.call-update
  8.0 0.7 fusion.6
  8.6 0.6 reduce-window.6
  9.2 0.2 slice_reduce_fusion
  9.4 0.8 fusion.5
  10.2 0.7 compare_select_fusion
  10.9 1.4 scatter_custom_fusion
  12.4 2.1 gather_fusion
  14.9 30.2 %all_to_all.15 = bf16[16,20,1024]{2,1,0:T(8,128)(2,1)S(1)} all-to-all(bf16[16,20,1024]{2,1,0:T(8,128)(2,1)S(1)} %broadcast_select_fusion), channel_id=1, replica_groups=mesh['dp'=16,'mp'=8,'section'=4] {'dp'}, dimensions={0} | all-to-all | bytes 1310720 | tf_op jit(solution)/shard_map/all_to_all | solution.py:102
  45.1 1.0 reshape.105
  46.1 0.7 all-gather.8.cloned.1.call-update
  46.8 1.4 gather_fusion.2
  48.3 0.8 broadcast_select_fusion.1
  49.0 5.9 all-to-all-start.2
  55.0 0.2 fusion.16
  55.3 8.2 all-to-all-done.2
  63.5 252.7 %all-gather.6.cloned.1.call-done = bf16[8192,128]{1,0:T(8,128)(2,1)} async-done(((bf16[128,128]{1,0:T(8,128)(2,1)}), bf16[8192,128]{1,0:T(8,128)(2,1)}) %all-gather.6.cloned.1.call-update) | async-done | bytes 2097168 | tf_op jit(solution)/shard_map/all_gather | solution.py:56
  316.1 64.4 %all-gather.4.cloned.1.call-done = bf16[320,8192]{1,0:T(8,128)(2,1)} async-done(((bf16[320,1024]{1,0:T(8,128)(2,1)}), bf16[320,8192]{1,0:T(8,128)(2,1)}) %all-gather.4.cloned.1.call-update) | async-done | bytes 5242896 | tf_op jit(solution)/shard_map/all_gather | solution.py:110
  380.6 4.8 fusion
  385.4 297.6 %all-gather.8.cloned.1.call-done = bf16[8192,128]{1,0:T(8,128)(2,1)} async-done(((bf16[128,128]{1,0:T(8,128)(2,1)}), bf16[8192,128]{1,0:T(8,128)(2,1)}) %all-gather.8.cloned.1.call-update) | async-done | bytes 2097168 | tf_op jit(solution)/shard_map/all_gather | solution.py:61
  683.0 4.8 fusion.1
  687.8 12.6 %all-reduce.1 = (f32[2,128]{1,0:T(2,128)S(1)}, f32[320]{0:T(512)S(1)}, f32[320]{0:T(512)S(1)}) all-reduce(f32[2,128]{1,0:T(2,128)S(1)} %bitcast.47, f32[320]{0:T(512)S(1)} %fusion.1, f32[320]{0:T(512)S(1)} %fusion), channel_id=1, replica_groups=mesh['dp'=16,'mp'=8,'section'=4] {'mp'}, use_global_device_ids=true, to_apply=%region_4.5 | all-reduce | flops 896 | bytes 7168 | tf_op jit(solution)/shard_map/psum | solution.py:95
  700.4 0.2 select_reduce_fusion.4
  700.7 8.3 all-reduce.2
  709.0 35.4 %all-reduce = (f32[16]{0:T(128)S(1)}, f32[16]{0:T(128)S(1)}) all-reduce(f32[16]{0:T(128)S(1)} %get-tuple-element.14, f32[16]{0:T(128)S(1)} %get-tuple-element.15), channel_id=1, replica_groups=mesh['dp'=16,'mp'=8,'section'=4] {'dp'}, use_global_device_ids=true, to_apply=%region_8.9 | all-reduce | flops 32 | bytes 256 | tf_op jit(solution)/shard_map/psum | solution.py:37
  744.3 0.2 select_reduce_fusion.2
  744.6 0.1 copy.22
  744.8 1.4 gather_fusion.1
  746.4 11.0 %all_to_all.16 = bf16[16,20,3]{1,2,0:T(4,128)(2,1)S(1)} all-to-all(bf16[16,20,3]{1,2,0:T(4,128)(2,1)S(1)} %copy.24), channel_id=1, replica_groups=mesh['dp'=16,'mp'=8,'section'=4] {'dp'}, dimensions={0} | all-to-all | bytes 3840 | tf_op jit(solution)/shard_map/all_to_all | solution.py:104
  757.6 6.5 fusion.2
  764.1 0.6 reshape.108
  764.7 320.1 %reduce-scatter.2.cloned.1.call-done = f32[128,128]{1,0:T(8,128)} async-done(((f32[8192,128]{1,0:T(8,128)}), f32[128,128]{1,0:T(8,128)}) %reduce-scatter.2.cloned.1.call-update) | async-done | bytes 65552 | tf_op jit(solution)/shard_map/reduce_scatter | solution.py:77
  (47 shorter events, 1.3 us)
Async XLA Ops:
  7.2 5.2 copy-start
  7.2 309.0 %all-gather.6.cloned.1.call-start = ((), (), s32[]{:S(2)}) async-start(), calls=%async_computation.5 | async-start | bytes 2129920 | tf_op jit(solution)/shard_map/all_gather | solution.py:56
  7.9 372.7 %all-gather.4.cloned.1.call-start = ((), (), s32[]{:S(2)}) async-start(), calls=%async_computation.4 | async-start | bytes 5898240 | tf_op jit(solution)/shard_map/all_gather | solution.py:110
  12.3 34.5 %copy-start.1 = (bf16[256,128]{1,0:T(8,128)(2,1)S(1)}, bf16[256,128]{1,0:T(8,128)(2,1)}, u32[]{:S(2)}) copy-start(bf16[256,128]{1,0:T(8,128)(2,1)} %param.10) | copy-start | bytes 196612
  14.5 40.5 %copy-start.2 = (bf16[1024]{0:T(1024)(128)(2,1)S(1)}, bf16[1024]{0:T(1024)(128)(2,1)}, u32[]{:S(2)}) copy-start(bf16[1024]{0:T(1024)(128)(2,1)} %param.15) | copy-start | bytes 6148
  14.5 40.5 %copy-start.5 = (bf16[256]{0:T(256)(128)(2,1)S(1)}, bf16[256]{0:T(256)(128)(2,1)}, u32[]{:S(2)}) copy-start(bf16[256]{0:T(256)(128)(2,1)} %param.11) | copy-start | bytes 1540
  14.5 40.8 %copy-start.4 = (s32[2]{0:T(128)S(1)}, s32[2]{0:T(128)}, u32[]{:S(2)}) copy-start(s32[2]{0:T(128)} %param.12) | copy-start | bytes 28
  46.1 636.9 %all-gather.8.cloned.1.call-start = ((), (), s32[]{:S(2)}) async-start(), calls=%async_computation.6 | async-start | bytes 2129920 | tf_op jit(solution)/shard_map/all_gather | solution.py:61
  49.0 14.5 %all-to-all-start.2 = ((bf16[16,20,128]{2,1,0:T(8,128)(2,1)}), bf16[16,20,128]{2,1,0:T(8,128)(2,1)S(1)}, u32[]{:S(2)}, u32[]{:S(2)}) async-start(bf16[16,20,128]{2,1,0:T(8,128)(2,1)} %broadcast_select_fusion.1), calls=%async_computation.2 | async-start | bytes 196608 | tf_op jit(solution)/shard_map/all_to_all | solution.py:103
  54.9 1029.9 %reduce-scatter.2.cloned.1.call-start = ((), (), s32[]{:S(2)}) async-start(), calls=%async_computation.7 | async-start | bytes 4259840 | tf_op jit(solution)/shard_map/reduce_scatter | solution.py:77
  385.4 315.2 %copy-start.3 = (s32[2]{0:T(128)S(1)}, s32[2]{0:T(128)}, u32[]{:S(2)}) copy-start(s32[2]{0:T(128)} %param.13) | copy-start | bytes 28
Sparse Core Ops, SparseCore 0:
  10.1 305.9 all-gather.5
  318.3 62.2 all-gather.3
  382.7 300.2 all-gather.7
  764.2 320.4 reduce-scatter.1
